TPU v7x, 32 devices: a whole 2x2x4 slice. The times are simulated.
32 devices in a mesh: ctx: 4 (over y, core), head: 2 (over x), dp: 4 (over z).
Axes of the slice: x: 2, y: 2, z: 4, core: 2. Of those that a mesh axis runs over, the one named last changes fastest.
Arguments:
- queries: bfloat16 [1024, 6144], P(('dp', 'ctx', 'head')), parts along dimension 0, may hold values from -18 to 18
- keys: bfloat16 [1024, 1024], P(('dp', 'ctx', 'head')), parts along dimension 0, may hold values from -9 to 9
- values: bfloat16 [1024, 1024], P(('dp', 'ctx', 'head')), parts along dimension 0, may hold values from -6 to 6
- level_gain: float32 [64, 6144], P(None, 'head'), may hold values from 0.5 to 4
- levels: int32 [16], P('dp'), parts along dimension 0, may hold values from 0 to 63
- visible: int32 [16, 4], P('dp'), parts along dimension 0, may hold values from 0 to 1, as said below
- counts: int32 [16], P('dp'), parts along dimension 0, may hold values from 32 to 64, as said below
Outputs:
- mixed: bfloat16 [1024, 6144], P(('dp', 'ctx', 'head')), parts along dimension 0
- finished: bfloat16 [256, 6144], P(('dp', 'ctx'), 'head'), parts along dimension 0
There are 4 independent parts, one for each index of `dp`. A program takes and returns all parts, laid end to end along the dimension named above; an argument that names none is the same for every part. Nothing has to cross between parts.
Inputs may be any that keep to these rules, and one draw needn't show every extreme that they name: visible[c][c] is 1, visible[c][d] is 0 for d > c, and entries below the diagonal are 0 or 1. `counts`: every clip has at least half of its slots live, and in every draw some clip has all 64 live.
All inputs are finite; a program needn't handle non-finite values.
Results may differ from a plain program's by a relative error of at most 0.0045.
Values may be sent and summed in bfloat16 or wider, within the bound.
No kernel may reach another device: no remote copies, remote signals or barrier semaphores. Data moves between devices by JAX's collectives and lax.ppermute only.
A program may use at most 64 MiB of HBM per device.

v0:
```python
import math
import jax
import jax.numpy as jnp
from jax import lax
from jax.sharding import PartitionSpec as P

QUERY_HEADS = 48
KEY_VALUE_HEADS = 8
HEAD_SIZE = 128
LEVELS = 64
CLIPS = 4


def from_behind(block, axis, distance):
    devices = range(lax.axis_size(axis))
    route = [(i - distance, i) for i in devices if i - distance in devices]
    return lax.ppermute(block, axis, route)


def body(queries, keys, values, level_gain, levels, visible, counts):
    head_count = lax.axis_size("head")
    ctx_count = lax.axis_size("ctx")
    ctx_index = lax.axis_index("ctx")
    tok_rows = queries.shape[0]
    rows_ctx = tok_rows * head_count
    clip_tok = rows_ctx * ctx_count // CLIPS
    heads_per_group = QUERY_HEADS // KEY_VALUE_HEADS
    scale = 1.0 / math.sqrt(HEAD_SIZE)
    clip_range = jnp.arange(CLIPS, dtype=jnp.int32)
    source_count = ctx_count // CLIPS
    query_local, key_local, value_local = (
        lax.all_to_all(queries, "head", split_axis=1, concat_axis=0, tiled=True),
        lax.all_to_all(keys, "head", split_axis=1, concat_axis=0, tiled=True),
        lax.all_to_all(values, "head", split_axis=1, concat_axis=0, tiled=True),
    )
    query_width = query_local.shape[1]
    query_ids = ctx_index * rows_ctx + jnp.arange(rows_ctx, dtype=jnp.int32)
    row_groups = [(0, rows_ctx)]
    query_grouped = query_local.reshape(rows_ctx, -1, heads_per_group, HEAD_SIZE)
    local_kv_heads = query_grouped.shape[1]
    query_onehot = (query_ids // clip_tok)[:, None] == clip_range[None, :]
    query_count = jnp.sum(jnp.where(query_onehot, counts[None, :], 0), axis=1)
    query_live = query_ids % clip_tok < query_count
    query_sees = jnp.sum(jnp.where(query_onehot[:, :, None], visible[None, :, :], 0), axis=1) == 1
    query_level = jnp.sum(jnp.where(query_onehot, levels[None, :], 0), axis=1)

    def key_block(carry_state, key_block_rows, value_block_rows, first_row):
        block_rows = key_block_rows.shape[0]
        key_ids = first_row + jnp.arange(block_rows, dtype=jnp.int32)
        key_onehot = (key_ids // clip_tok)[:, None] == clip_range[None, :]
        key_count = jnp.sum(jnp.where(key_onehot, counts[None, :], 0), axis=1)
        key_live = key_ids % clip_tok < key_count
        block_clips = jnp.any(key_onehot & key_live[:, None], axis=0)
        key_head_rows = key_block_rows.reshape(block_rows, -1, HEAD_SIZE)
        value_head_rows = value_block_rows.reshape(block_rows, -1, HEAD_SIZE)
        group_start, group_rows = row_groups[0]
        group_end = group_start + group_rows
        part_state = tuple((member for member in carry_state))
        group_sees = query_sees
        needed = jnp.any(jnp.any(group_sees, axis=0) & block_clips)

        def update(state, group_sees=group_sees, group_start=group_start, group_end=group_end):
            running_max, denominator, weighted = state
            allowed = (
                jnp.any(group_sees[:, None, :] & key_onehot[None, :, :], axis=-1)
                & key_live[None, :]
            )
            scores = (
                jnp.einsum(
                    "rkgd,nkd->rkgn",
                    query_grouped,
                    key_head_rows,
                    preferred_element_type=jnp.float32,
                )
                * scale
            )
            key_mask = allowed[:, None, None, :]
            scores = jnp.where(key_mask, scores, -1e30)
            new_max = jnp.maximum(running_max, jnp.max(scores, axis=-1))
            weights = jnp.where(key_mask, jnp.exp(scores - new_max[..., None]), 0.0)
            shrink = jnp.exp(running_max - new_max)
            denominator = denominator * shrink + jnp.sum(weights, axis=-1)
            weighted = weighted * shrink[..., None] + jnp.einsum(
                "rkgn,nkd->rkgd",
                weights.astype(jnp.bfloat16),
                value_head_rows,
                preferred_element_type=jnp.float32,
            )
            return (new_max, denominator, weighted)

        def keep(state):
            return state

        group_states = [lax.cond(needed, update, keep, part_state)]
        if len(group_states) == 1:
            return group_states[0]
        return tuple(
            (
                jnp.concatenate([state[member] for state in group_states], axis=0)
                for member in range(3)
            )
        )

    initial = (
        jnp.full((rows_ctx, local_kv_heads, heads_per_group), -1e30, jnp.float32),
        jnp.zeros((rows_ctx, local_kv_heads, heads_per_group), jnp.float32),
        jnp.zeros((rows_ctx, local_kv_heads, heads_per_group, HEAD_SIZE), jnp.float32),
    )
    key_piece = lax.all_gather(key_local, "ctx", axis=0, tiled=True)
    value_piece = lax.all_gather(value_local, "ctx", axis=0, tiled=True)
    piece_rows = key_piece.shape[0]
    block_rows = math.gcd(piece_rows, 512)

    def advance(block_index, inner_state):
        key_slice = lax.dynamic_slice_in_dim(key_piece, block_index * block_rows, block_rows, 0)
        value_slice = lax.dynamic_slice_in_dim(value_piece, block_index * block_rows, block_rows, 0)
        return key_block(inner_state, key_slice, value_slice, block_index * block_rows)

    final_state = lax.fori_loop(0, piece_rows // block_rows, advance, initial)
    attended = (final_state[2] / final_state[1][..., None]).reshape(rows_ctx, query_width)
    level_onehot = (query_level[:, None] == jnp.arange(LEVELS, dtype=jnp.int32)[None, :]).astype(
        jnp.float32
    )
    gate_rows = jnp.dot(
        level_onehot,
        level_gain,
        precision=lax.Precision.HIGHEST,
        preferred_element_type=jnp.float32,
    )
    gated = jnp.where(query_live[:, None], attended * gate_rows, 0.0).astype(jnp.bfloat16)
    mixed = lax.all_to_all(gated, "head", split_axis=0, concat_axis=1, tiled=True)
    relay_rows = rows_ctx // CLIPS
    held = jnp.where(ctx_index < source_count, gated, jnp.zeros_like(gated)).reshape(
        CLIPS, relay_rows, query_width
    )
    empty_block = jnp.zeros_like(held)
    sources = jnp.arange(source_count, dtype=jnp.int32)
    hop_bits = (source_count - 1).bit_length()
    for bit_number in reversed(range(hop_bits)):
        higher = sources >> bit_number + 1 << bit_number + 1
        places = sources + 3 * higher
        holds_bit = jnp.any((places == ctx_index) & (sources >> bit_number & 1 == 1))
        moving = jnp.where(holds_bit, held, empty_block)
        staying = jnp.where(holds_bit, empty_block, held)
        arriving = from_behind(moving, "ctx", 3 * (1 << bit_number))
        held = staying + arriving
    group_position = ctx_index % CLIPS
    finished = held[0]
    for lane_number in range(1, CLIPS):
        arriving_tile = from_behind(held[lane_number], "ctx", lane_number)
        finished = jnp.where(group_position == lane_number, arriving_tile, finished)
    return (mixed, finished)


def solution(mesh):
    placed = (
        P(("dp", "ctx", "head"), None),
        P(("dp", "ctx", "head"), None),
        P(("dp", "ctx", "head"), None),
        P(None, "head"),
        P("dp"),
        P("dp", None),
        P("dp"),
    )
    return jax.shard_map(
        body,
        mesh=mesh,
        in_specs=placed,
        out_specs=(P(("dp", "ctx", "head"), None), P(("dp", "ctx"), "head")),
        check_vma=False,
    )
```

profile of v0, /device:TPU:0, one launch (start us, length us, event | category | flops | bytes accessed | tf_op | source)
XLA Modules:
  0.0 61.5 jit_solution(9454937511669953927)
XLA Ops:
  0.6 1.5 %copy.71 = bf16[4,2,8,512]{3,2,0,1:T(8,128)(2,1)} copy(bf16[4,2,8,512]{3,2,1,0:T(8,128)(2,1)} %bitcast.40) | data formatting | bytes 131072 | tf_op jit(solution)/shard_map/all_to_all | solution.py:33
  2.2 4.2 %all-to-all-start = ((bf16[32,2,512]{2,0,1:T(8,128)(2,1)}), bf16[32,2,512]{2,0,1:T(8,128)(2,1)S(1)}, u32[]{:S(2)}, u32[]{:S(2)}) async-start(bf16[32,2,512]{2,0,1:T(8,128)(2,1)} %bitcast.31), calls=%async_computation | async-start | bytes 131072 | tf_op jit(solution)/shard_map/all_to_all | solution.py:33
  6.5 0.8 %select_reduce_fusion = s32[64,4]{0,1:T(4,128)S(1)} fusion(s32[4,4]{1,0:T(4,128)} %param.14, pred[64,4]{0,1:T(4,128)(4,1)S(1)} %iota_compare_fusion.3), kind=kLoop, calls=%fused_computation.33 | loop fusion | flops 1792 | bytes 1344 | tf_op jit(solution)/shard_map/reduce_sum | solution.py:44
  7.3 0.7 %select_reduce_fusion.1 = s32[256]{0:T(256)S(1)} fusion(s32[4]{0:T(128)} %param.15, s32[256]{0:T(256)S(1)} %and_select_fusion.2), kind=kLoop, calls=%fused_computation.34 | loop fusion | flops 2816 | bytes 2064 | tf_op jit(solution)/shard_map/while/body/eval_jaxpr/reduce_sum | solution.py:51
  8.1 0.1 iota_compare_fusion.2
  8.2 0.8 %select_reduce_fusion.2 = (s32[64]{0:T(128)S(1)}, s32[64]{0:T(128)S(1)}) fusion(s32[4]{0:T(128)} %param.13, s32[64]{0:T(128)S(1)} %and_select_fusion.3, s32[4]{0:T(128)} %param.15), kind=kLoop, calls=%fused_computation.37 | loop fusion | flops 1152 | bytes 800 | tf_op jit(solution)/shard_map/reduce_sum | solution.py:45
  9.0 0.6 %and_reduce_fusion.2 = pred[]{:T(512)} fusion(pred[4]{0:T(512)(128)(4,1)S(1)} %get-tuple-element.148, pred[4]{0:T(512)(128)(4,1)S(1)} %get-tuple-element.158), kind=kLoop, calls=%fused_computation.43 | loop fusion | flops 7 | bytes 9 | tf_op jit(solution)/shard_map/while/body/eval_jaxpr/reduce_or | solution.py:60
  9.6 1.5 %copy.70 = bf16[4,2,8,512]{3,2,0,1:T(8,128)(2,1)} copy(bf16[4,2,8,512]{3,2,1,0:T(8,128)(2,1)} %bitcast.41) | data formatting | bytes 131072 | tf_op jit(solution)/shard_map/all_to_all | solution.py:34
  11.1 3.3 %all-to-all-start.2 = ((bf16[32,2,512]{2,0,1:T(8,128)(2,1)}), bf16[32,2,512]{2,0,1:T(8,128)(2,1)S(1)}, u32[]{:S(2)}, u32[]{:S(2)}) async-start(bf16[32,2,512]{2,0,1:T(8,128)(2,1)} %bitcast.30), calls=%async_computation.2 | async-start | bytes 131072 | tf_op jit(solution)/shard_map/all_to_all | solution.py:34
  15.1 1.8 %copy.69 = bf16[4,2,8,3072]{3,2,0,1:T(8,128)(2,1)} copy(bf16[4,2,8,3072]{3,2,1,0:T(8,128)(2,1)} %bitcast.35) | data formatting | bytes 786432 | tf_op jit(solution)/shard_map/all_to_all | solution.py:32
  16.9 1.6 %all-to-all-done.2 = bf16[32,2,512]{2,0,1:T(8,128)(2,1)S(1)} async-done(((bf16[32,2,512]{2,0,1:T(8,128)(2,1)}), bf16[32,2,512]{2,0,1:T(8,128)(2,1)S(1)}, u32[]{:S(2)}, u32[]{:S(2)}) %all-to-all-start.2) | async-done | bytes 65568 | tf_op jit(solution)/shard_map/all_to_all | solution.py:34
  18.5 3.5 %all-to-all-start.1 = ((bf16[32,2,3072]{2,0,1:T(8,128)(2,1)}), bf16[32,2,3072]{2,0,1:T(8,128)(2,1)S(1)}, u32[]{:S(2)}, u32[]{:S(2)}) async-start(bf16[32,2,3072]{2,0,1:T(8,128)(2,1)} %bitcast.29), calls=%async_computation.1 | async-start | bytes 786432 | tf_op jit(solution)/shard_map/all_to_all | solution.py:32
  22.0 6.3 %all_gather.6 = bf16[256,512]{1,0:T(8,128)(2,1)S(1)} all-gather(bf16[64,512]{1,0:T(8,128)(2,1)S(1)} %bitcast.37), channel_id=1, replica_groups=mesh['ctx'=4,'head'=2,'dp'=4] {'ctx'}, dimensions={0}, use_global_device_ids=true | all-gather | bytes 327680 | tf_op jit(solution)/shard_map/all_gather | solution.py:109
  28.3 5.8 %all_gather.7 = bf16[256,512]{1,0:T(8,128)(2,1)S(1)} all-gather(bf16[64,512]{1,0:T(8,128)(2,1)S(1)} %bitcast.38), channel_id=1, replica_groups=mesh['ctx'=4,'head'=2,'dp'=4] {'ctx'}, dimensions={0}, use_global_device_ids=true | all-gather | bytes 327680 | tf_op jit(solution)/shard_map/all_gather | solution.py:110
  34.2 6.7 %conditional.1 = ((f32[64,4,6]{0,2,1:T(8,128)S(1)}, f32[64,4,6,128]{3,0,2,1:T(8,128)S(1)})) conditional(s32[]{:T(128)} %convert_element_type.13, (f32[64,4,6]{0,2,1:T(8,128)S(1)}, f32[64,4,6,128]{3,0,2,1:T(8,128)S(1)}) %tuple.31, (pred[64,4]{0,1:T(4,128)(4,1)S(1)}, pred[256,4]{0,1:T(4,128)(4,1)S(1)}, s32[256]{0:T(256)S(1)}, s32[256]{0:T(256)S(1)}, ...), branch_computations={%region_6.7_spmd, %region_7.11_spmd} | conditional | flops 205395968 | bytes 9220888 | solution.py:94
  34.2 1.3 %reshape.148 = bf16[64,4,6,128]{3,2,1,0:T(8,128)(2,1)} reshape(bf16[2,32,3072]{2,1,0:T(8,128)(2,1)S(1)} %get-tuple-element.127) | data formatting | bytes 786432 | tf_op jit(solution)/shard_map/reshape | solution.py:39
  35.4 0.8 %reshape.147 = bf16[256,4,128]{2,1,0:T(4,128)(2,1)} reshape(bf16[256,512]{1,0:T(8,128)(2,1)S(1)} %get-tuple-element.126) | data formatting | bytes 524288 | tf_op jit(solution)/shard_map/while/body/eval_jaxpr/reshape | solution.py:54
  36.4 1.6 %fusion.21 = (f32[64,4,6]{0,2,1:T(8,128)S(1)}, f32[64,4,6,256]{3,0,2,1:T(8,128)S(1)}) fusion(bf16[64,4,6,128]{3,2,1,0:T(8,128)(2,1)} %reshape.148, bf16[256,4,128,1]{2,1,0,3:T(4,128)(2,1)} %bitcast.39, pred[64,256]{1,0:T(8,128)(4,1)S(1)} %broadcast_and_fusion), kind=kOutput, calls=%fused_computation.57 | convolution fusion | flops 101841408 | bytes 2250752 | tf_op jit(solution)/shard_map/while/body/eval_jaxpr/cond/branch_1_fun/rkgd,nkd->rkgn/dot_general | solution.py:69
  38.0 0.5 fusion.2
  38.6 0.8 %reshape.149 = bf16[256,4,128]{2,1,0:T(4,128)(2,1)} reshape(bf16[256,512]{1,0:T(8,128)(2,1)S(1)} %get-tuple-element.129) | data formatting | bytes 524288 | tf_op jit(solution)/shard_map/while/body/eval_jaxpr/reshape | solution.py:55
  39.3 1.6 %fusion = f32[64,4,6,128]{3,0,2,1:T(8,128)S(1)} fusion(f32[64,4,6,256]{3,0,2,1:T(8,128)S(1)} %get-tuple-element.153, f32[64,4,6,128]{3,0,2,1:T(8,128)S(1)} %get-tuple-element.128, f32[64,4,6]{0,2,1:T(8,128)S(1)} %broadcast_maximum_fusion, pred[64,256]{1,0:T(8,128)(4,1)S(1)} %broadcast_and_fusion, f32[64,4,6]{0,2,1:T(8,128)S(1)} %get-tuple-element.150, ...), kind=kOutput, calls=%fused_computation.3 | convolution fusion | flops 102236160 | bytes 3436544 | tf_op jit(solution)/shard_map/while/body/eval_jaxpr/cond/branch_1_fun/rkgn,nkd->rkgd/dot_general | solution.py:83
  40.9 0.3 broadcast_divide_fusion
  41.2 0.5 copy.44
  41.7 0.2 reshape.151
  41.9 1.3 %broadcast_select_fusion = (bf16[64,3072]{1,0:T(8,128)(2,1)S(1)}, bf16[64,3072]{1,0:T(8,128)(2,1)}) fusion(pred[]{:T(512)S(6)} %lt.53, f32[64,3072]{1,0:T(8,128)S(1)} %reshape.151, f32[64,3072]{1,0:T(8,128)S(1)} %copy-done, s32[64]{0:T(128)S(1)} %get-tuple-element.146, pred[64]{0:T(512)(128)(4,1)S(1)} %fusion.19), kind=kOutput, calls=%fused_computation.25 | convolution fusion | flops 151785472 | bytes 2359617 | tf_op jit(solution)/shard_map/dot_general | solution.py:124
  43.2 3.4 %collective-permute-start = (bf16[16,3072]{1,0:T(8,128)(2,1)S(1)}, bf16[16,3072]{1,0:T(8,128)(2,1)S(1)}, u32[]{:S(2)}, u32[]{:S(2)}) collective-permute-start(bf16[16,3072]{1,0:T(8,128)(2,1)S(1)} %get-tuple-element.156), channel_id=1, source_target_pairs={{0,24},{1,25},{2,26},{3,27},{4,28},{5,29},{6,30},{7,31}} | collective-permute-start | bytes 294920 | tf_op jit(solution)/shard_map/ppermute | solution.py:17
  46.6 1.3 %collective-permute-start.1 = (bf16[16,3072]{1,0:T(8,128)(2,1)S(1)}, bf16[16,3072]{1,0:T(8,128)(2,1)S(1)}, u32[]{:S(2)}, u32[]{:S(2)}) collective-permute-start(bf16[16,3072]{1,0:T(8,128)(2,1)S(1)} %get-tuple-element.155), channel_id=1, source_target_pairs={{0,16},{8,24},{1,17},{9,25},{2,18},{10,26},{3,19},{11,27},{4,20},{... | collective-permute-start | bytes 294920 | tf_op jit(solution)/shard_map/ppermute | solution.py:17
  47.9 2.0 %collective-permute-start.2 = (bf16[16,3072]{1,0:T(8,128)(2,1)S(1)}, bf16[16,3072]{1,0:T(8,128)(2,1)S(1)}, u32[]{:S(2)}, u32[]{:S(2)}) collective-permute-start(bf16[16,3072]{1,0:T(8,128)(2,1)S(1)} %get-tuple-element.154), channel_id=1, source_target_pairs={{0,8},{8,16},{16,24},{1,9},{9,17},{17,25},{2,10},{10,18},{18,26},{... | collective-permute-start | bytes 294920 | tf_op jit(solution)/shard_map/ppermute | solution.py:17
  50.0 3.5 %all-to-all-start.3 = ((bf16[2,32,3072]{2,1,0:T(8,128)(2,1)}), bf16[2,32,3072]{2,1,0:T(8,128)(2,1)S(1)}, u32[]{:S(2)}, u32[]{:S(2)}) async-start(bf16[2,32,3072]{2,1,0:T(8,128)(2,1)} %bitcast.9), calls=%async_computation.3 | async-start | bytes 786432 | tf_op jit(solution)/shard_map/all_to_all | solution.py:131
  53.5 0.7 %fusion.15 = bf16[16,3072]{1,0:T(8,128)(2,1)} fusion(bf16[16,3072]{1,0:T(8,128)(2,1)S(1)} %collective-permute-done, bf16[16,3072]{1,0:T(8,128)(2,1)S(1)} %collective-permute-done.1, bf16[16,3072]{1,0:T(8,128)(2,1)S(1)} %collective-permute-done.2, bf16[64,3072]{1,0:T(8,128)(2,1)S(1)} %get-tuple-element.159, pred[]{:T(512)S(6)} %eq.97, pred[]{:T(512)S(6)} %eq.96, ...), kind=kLoop, calls=%fused_computation.28 | loop fusion | flops 147456 | bytes 491523 | tf_op jit(solution)/shard_map/jit(_where)/select_n | solution.py:151
  54.1 6.6 %all-to-all-done.3 = bf16[2,32,3072]{2,1,0:T(8,128)(2,1)S(1)} async-done(((bf16[2,32,3072]{2,1,0:T(8,128)(2,1)}), bf16[2,32,3072]{2,1,0:T(8,128)(2,1)S(1)}, u32[]{:S(2)}, u32[]{:S(2)}) %all-to-all-start.3) | async-done | bytes 393248 | tf_op jit(solution)/shard_map/all_to_all | solution.py:131
  60.7 0.8 %copy.55 = bf16[2,4,8,3072]{3,2,0,1:T(8,128)(2,1)} copy(bf16[2,4,8,3072]{3,2,1,0:T(8,128)(2,1)S(1)} %bitcast.33) | data formatting | bytes 786432 | tf_op jit(solution)/shard_map/all_to_all | solution.py:131
  (23 shorter events, 0.4 us)
Async XLA Ops:
  0.6 41.2 %copy-start = (f32[64,3072]{1,0:T(8,128)S(1)}, f32[64,3072]{1,0:T(8,128)}, u32[]{:S(2)}) copy-start(f32[64,3072]{1,0:T(8,128)} %param.12) | copy-start | bytes 2359300
  2.2 8.9 %all-to-all-start = ((bf16[32,2,512]{2,0,1:T(8,128)(2,1)}), bf16[32,2,512]{2,0,1:T(8,128)(2,1)S(1)}, u32[]{:S(2)}, u32[]{:S(2)}) async-start(bf16[32,2,512]{2,0,1:T(8,128)(2,1)} %bitcast.31), calls=%async_computation | async-start | bytes 131072 | tf_op jit(solution)/shard_map/all_to_all | solution.py:33
  11.1 7.4 %all-to-all-start.2 = ((bf16[32,2,512]{2,0,1:T(8,128)(2,1)}), bf16[32,2,512]{2,0,1:T(8,128)(2,1)S(1)}, u32[]{:S(2)}, u32[]{:S(2)}) async-start(bf16[32,2,512]{2,0,1:T(8,128)(2,1)} %bitcast.30), calls=%async_computation.2 | async-start | bytes 131072 | tf_op jit(solution)/shard_map/all_to_all | solution.py:34
  18.5 15.6 %all-to-all-start.1 = ((bf16[32,2,3072]{2,0,1:T(8,128)(2,1)}), bf16[32,2,3072]{2,0,1:T(8,128)(2,1)S(1)}, u32[]{:S(2)}, u32[]{:S(2)}) async-start(bf16[32,2,3072]{2,0,1:T(8,128)(2,1)} %bitcast.29), calls=%async_computation.1 | async-start | bytes 786432 | tf_op jit(solution)/shard_map/all_to_all | solution.py:32
  43.2 10.2 %collective-permute-start = (bf16[16,3072]{1,0:T(8,128)(2,1)S(1)}, bf16[16,3072]{1,0:T(8,128)(2,1)S(1)}, u32[]{:S(2)}, u32[]{:S(2)}) collective-permute-start(bf16[16,3072]{1,0:T(8,128)(2,1)S(1)} %get-tuple-element.156), channel_id=1, source_target_pairs={{0,24},{1,25},{2,26},{3,27},{4,28},{5,29},{6,30},{7,31}} | collective-permute-start | bytes 294920 | tf_op jit(solution)/shard_map/ppermute | solution.py:17
  46.6 6.8 %collective-permute-start.1 = (bf16[16,3072]{1,0:T(8,128)(2,1)S(1)}, bf16[16,3072]{1,0:T(8,128)(2,1)S(1)}, u32[]{:S(2)}, u32[]{:S(2)}) collective-permute-start(bf16[16,3072]{1,0:T(8,128)(2,1)S(1)} %get-tuple-element.155), channel_id=1, source_target_pairs={{0,16},{8,24},{1,17},{9,25},{2,18},{10,26},{3,19},{11,27},{4,20},{... | collective-permute-start | bytes 294920 | tf_op jit(solution)/shard_map/ppermute | solution.py:17
  47.9 5.6 %collective-permute-start.2 = (bf16[16,3072]{1,0:T(8,128)(2,1)S(1)}, bf16[16,3072]{1,0:T(8,128)(2,1)S(1)}, u32[]{:S(2)}, u32[]{:S(2)}) collective-permute-start(bf16[16,3072]{1,0:T(8,128)(2,1)S(1)} %get-tuple-element.154), channel_id=1, source_target_pairs={{0,8},{8,16},{16,24},{1,9},{9,17},{17,25},{2,10},{10,18},{18,26},{... | collective-permute-start | bytes 294920 | tf_op jit(solution)/shard_map/ppermute | solution.py:17
  50.0 10.7 %all-to-all-start.3 = ((bf16[2,32,3072]{2,1,0:T(8,128)(2,1)}), bf16[2,32,3072]{2,1,0:T(8,128)(2,1)S(1)}, u32[]{:S(2)}, u32[]{:S(2)}) async-start(bf16[2,32,3072]{2,1,0:T(8,128)(2,1)} %bitcast.9), calls=%async_computation.3 | async-start | bytes 786432 | tf_op jit(solution)/shard_map/all_to_all | solution.py:131
where the time goes:
time: 62.2 us; the launch traced here: 61.5 us
  starting transfers between devices  21.2 us (34%)
  blocking collectives  12.1 us (19%)
  local copies, waits for them, and re-layouts  9.12 us (15%)
  waiting for transfers between devices  8.19 us (13%)
  other arithmetic  4.82 us (8%)
  matrix products  4.5 us (7%)
  between operations  1.43 us (2%)
    ppermute x3, starting transfers between devices, from_behind(): return lax.ppermute(block, axis, route)  6.7 us
    all_to_all x1, waiting for transfers between devices, body(): lax.all_to_all(gated, 'head', split_axis=0, concat_axis=1, tiled=True)  6.56 us
    all_gather x1, blocking collectives, body(): key_piece = lax.all_gather(key_local, 'ctx', axis=0, tiled=True)  6.31 us
    all_gather x1, blocking collectives, body(): value_piece = lax.all_gather(value_local, 'ctx', axis=0, tiled=True)  5.84 us
    all_to_all x1, starting transfers between devices, body(): lax.all_to_all(keys, 'head', split_axis=1, concat_axis=0, tiled=True)  4.23 us
    all_to_all x1, starting transfers between devices, body(): lax.all_to_all(gated, 'head', split_axis=0, concat_axis=1, tiled=True)  3.48 us
    all_to_all x1, starting transfers between devices, body(): lax.all_to_all(queries, 'head', split_axis=1, concat_axis=0, tiled=True)  3.47 us
    all_to_all x1, starting transfers between devices, body(): lax.all_to_all(values, 'head', split_axis=1, concat_axis=0, tiled=True)  3.32 us
  transfers between devices with their start and end apart: 7, of which 2 were waited for; matrix products, arithmetic and copies ran while one was open for 12% of the time, Pallas kernels for 0%

commit v1 on v0

--- a/solution.py
+++ b/solution.py
@@ -106,8 +106,13 @@
         jnp.zeros((rows_ctx, local_kv_heads, heads_per_group), jnp.float32),
         jnp.zeros((rows_ctx, local_kv_heads, heads_per_group, HEAD_SIZE), jnp.float32),
     )
-    key_piece = lax.all_gather(key_local, "ctx", axis=0, tiled=True)
-    value_piece = lax.all_gather(value_local, "ctx", axis=0, tiled=True)
+    key_piece, value_piece = jnp.split(
+        lax.all_gather(
+            jnp.concatenate([key_local, value_local], axis=1), "ctx", axis=0, tiled=True
+        ),
+        [key_local.shape[1]],
+        axis=1,
+    )
     piece_rows = key_piece.shape[0]
     block_rows = math.gcd(piece_rows, 512)
 

time: 62.2 us -> 53 us (0.85)
  blocking collectives: 12.1 us -> 7.73 us
  local copies, waits for them, and re-layouts: 9.12 us -> 7.04 us
  matrix products: 4.5 us -> 2.46 us
  starting transfers between devices: 21.2 us -> 20.5 us
    all_gather x2 -> x1, blocking collectives: 12.1 us -> 7.73 us  [body(): lax.all_gather(jnp.concatenate([key_local, value_local], axis=1), 'ctx',...]
    all_to_all x1, waiting for transfers between devices: 0.01 us -> 1.61 us  [body(): lax.all_to_all(keys, 'head', split_axis=1, concat_axis=0, tiled=True)]
    all_to_all x1, waiting for transfers between devices: 1.61 us -> 0.01 us  [body(): lax.all_to_all(values, 'head', split_axis=1, concat_axis=0, tiled=True)]
    reshape x2 -> x0, local copies, waits for them, and re-layouts: 1.53 us -> none  [the longest x1 0.77 us: key_block(): value_head_rows = value_block_rows.reshape(block_rows, -1, HEAD_SIZE)]
    dot_general x1, matrix products: 1.63 us -> 0.48 us  [update(): jnp.einsum('rkgd,nkd->rkgn', query_grouped, key_head_rows, preferred_elem...]
    all_to_all x1, starting transfers between devices: 4.23 us -> 3.32 us  [body(): lax.all_to_all(keys, 'head', split_axis=1, concat_axis=0, tiled=True)]
    all_to_all x1, starting transfers between devices: 3.32 us -> 4.23 us  [body(): lax.all_to_all(values, 'head', split_axis=1, concat_axis=0, tiled=True)]
    dot_general x1, matrix products: 1.56 us -> 0.67 us  [update(): jnp.einsum('rkgn,nkd->rkgd', weights.astype(jnp.bfloat16), value_head_row...]
  transfers between devices with their start and end apart: 7 -> 7, of which waited for: 2 -> 2; matrix products, arithmetic and copies ran while one was open for 12% -> 14% of each run, Pallas kernels for 0% -> 0%
where the time goes in v1:
time: 53 us; the launch traced here: 52.3 us
  starting transfers between devices  20.5 us (39%)
  waiting for transfers between devices  8.22 us (16%)
  blocking collectives  7.73 us (15%)
  local copies, waits for them, and re-layouts  7.04 us (13%)
  other arithmetic  4.85 us (9%)
  matrix products  2.46 us (5%)
  between operations  1.44 us (3%)
    all_gather x1, blocking collectives, body(): lax.all_gather(jnp.concatenate([key_local, value_local], axis=1), 'ctx',...  7.73 us
    all_to_all x1, waiting for transfers between devices, body(): lax.all_to_all(gated, 'head', split_axis=0, concat_axis=1, tiled=True)  6.59 us
    ppermute x3, starting transfers between devices, from_behind(): return lax.ppermute(block, axis, route)  6 us
    all_to_all x1, starting transfers between devices, body(): lax.all_to_all(values, 'head', split_axis=1, concat_axis=0, tiled=True)  4.23 us
    all_to_all x1, starting transfers between devices, body(): lax.all_to_all(gated, 'head', split_axis=0, concat_axis=1, tiled=True)  3.48 us
    all_to_all x1, starting transfers between devices, body(): lax.all_to_all(queries, 'head', split_axis=1, concat_axis=0, tiled=True)  3.47 us
    all_to_all x1, starting transfers between devices, body(): lax.all_to_all(keys, 'head', split_axis=1, concat_axis=0, tiled=True)  3.32 us
    all_to_all x1, local copies, waits for them, and re-layouts, body(): lax.all_to_all(queries, 'head', split_axis=1, concat_axis=0, tiled=True)  1.77 us
  transfers between devices with their start and end apart: 7, of which 2 were waited for; matrix products, arithmetic and copies ran while one was open for 14% of the time, Pallas kernels for 0%

profile of v1, /device:TPU:0, one launch (start us, length us, event | category | flops | bytes accessed | tf_op | source)
XLA Modules:
  0.0 52.3 jit_solution(1430453020769166919)
XLA Ops:
  0.6 1.5 %copy.84 = bf16[4,2,8,512]{3,2,0,1:T(8,128)(2,1)} copy(bf16[4,2,8,512]{3,2,1,0:T(8,128)(2,1)} %bitcast.50) | data formatting | bytes 131072 | tf_op jit(solution)/shard_map/all_to_all | solution.py:34
  2.2 4.2 %all-to-all-start.1 = ((bf16[32,2,512]{2,0,1:T(8,128)(2,1)}), bf16[32,2,512]{2,0,1:T(8,128)(2,1)S(1)}, u32[]{:S(2)}, u32[]{:S(2)}) async-start(bf16[32,2,512]{2,0,1:T(8,128)(2,1)} %bitcast.40), calls=%async_computation.1 | async-start | bytes 131072 | tf_op jit(solution)/shard_map/all_to_all | solution.py:34
  6.5 0.8 %select_reduce_fusion = s32[64,4]{0,1:T(4,128)S(1)} fusion(s32[4,4]{1,0:T(4,128)} %param.14, pred[64,4]{0,1:T(4,128)(4,1)S(1)} %iota_compare_fusion.3), kind=kLoop, calls=%fused_computation.32 | loop fusion | flops 1792 | bytes 1344 | tf_op jit(solution)/shard_map/reduce_sum | solution.py:44
  7.2 0.1 fusion.18
  7.3 0.7 %select_reduce_fusion.1 = s32[256]{0:T(256)S(1)} fusion(s32[4]{0:T(128)} %param.15, s32[256]{0:T(256)S(1)} %and_select_fusion.2), kind=kLoop, calls=%fused_computation.33 | loop fusion | flops 2816 | bytes 2064 | tf_op jit(solution)/shard_map/while/body/eval_jaxpr/reduce_sum | solution.py:51
  8.1 0.1 iota_compare_fusion.2
  8.2 0.8 %select_reduce_fusion.2 = (s32[64]{0:T(128)S(1)}, s32[64]{0:T(128)S(1)}) fusion(s32[4]{0:T(128)} %param.13, s32[64]{0:T(128)S(1)} %and_select_fusion.3, s32[4]{0:T(128)} %param.15), kind=kLoop, calls=%fused_computation.36 | loop fusion | flops 1152 | bytes 800 | tf_op jit(solution)/shard_map/reduce_sum | solution.py:45
  9.0 0.6 %and_reduce_fusion.2 = pred[]{:T(512)} fusion(pred[4]{0:T(512)(128)(4,1)S(1)} %get-tuple-element.183, pred[4]{0:T(512)(128)(4,1)S(1)} %get-tuple-element.195), kind=kLoop, calls=%fused_computation.42 | loop fusion | flops 7 | bytes 9 | tf_op jit(solution)/shard_map/while/body/eval_jaxpr/reduce_or | solution.py:60
  9.6 1.5 %copy.85 = bf16[4,2,8,512]{3,2,0,1:T(8,128)(2,1)} copy(bf16[4,2,8,512]{3,2,1,0:T(8,128)(2,1)} %bitcast.51) | data formatting | bytes 131072 | tf_op jit(solution)/shard_map/all_to_all | solution.py:33
  11.1 3.3 %all-to-all-start = ((bf16[32,2,512]{2,0,1:T(8,128)(2,1)}), bf16[32,2,512]{2,0,1:T(8,128)(2,1)S(1)}, u32[]{:S(2)}, u32[]{:S(2)}) async-start(bf16[32,2,512]{2,0,1:T(8,128)(2,1)} %bitcast.41), calls=%async_computation | async-start | bytes 131072 | tf_op jit(solution)/shard_map/all_to_all | solution.py:33
  15.1 1.8 %copy.83 = bf16[4,2,8,3072]{3,2,0,1:T(8,128)(2,1)} copy(bf16[4,2,8,3072]{3,2,1,0:T(8,128)(2,1)} %bitcast.46) | data formatting | bytes 786432 | tf_op jit(solution)/shard_map/all_to_all | solution.py:32
  16.9 1.6 %all-to-all-done = bf16[32,2,512]{2,0,1:T(8,128)(2,1)S(1)} async-done(((bf16[32,2,512]{2,0,1:T(8,128)(2,1)}), bf16[32,2,512]{2,0,1:T(8,128)(2,1)S(1)}, u32[]{:S(2)}, u32[]{:S(2)}) %all-to-all-start) | async-done | bytes 65568 | tf_op jit(solution)/shard_map/all_to_all | solution.py:33
  18.5 3.5 %all-to-all-start.2 = ((bf16[32,2,3072]{2,0,1:T(8,128)(2,1)}), bf16[32,2,3072]{2,0,1:T(8,128)(2,1)S(1)}, u32[]{:S(2)}, u32[]{:S(2)}) async-start(bf16[32,2,3072]{2,0,1:T(8,128)(2,1)} %bitcast.39), calls=%async_computation.2 | async-start | bytes 786432 | tf_op jit(solution)/shard_map/all_to_all | solution.py:32
  22.0 7.7 %all_gather.3 = bf16[256,1024]{1,0:T(8,128)(2,1)S(1)} all-gather(bf16[64,1024]{1,0:T(8,128)(2,1)S(1)} %pad_maximum_fusion), channel_id=1, replica_groups=mesh['ctx'=4,'head'=2,'dp'=4] {'ctx'}, dimensions={0}, use_global_device_ids=true | all-gather | bytes 655360 | tf_op jit(solution)/shard_map/all_gather | solution.py:110
  29.8 2.6 %conditional.1 = ((f32[64,4,6]{0,2,1:T(8,128)S(1)}, f32[64,4,6,128]{3,0,2,1:T(8,128)S(1)})) conditional(s32[]{:T(128)} %convert_element_type.13, (f32[64,4,6]{0,2,1:T(8,128)S(1)}, f32[64,4,6,128]{3,0,2,1:T(8,128)S(1)}) %tuple.32, (pred[64,4]{0,1:T(4,128)(4,1)S(1)}, pred[256,4]{0,1:T(4,128)(4,1)S(1)}, s32[256]{0:T(256)S(1)}, s32[256]{0:T(256)S(1)}, ...), branch_computations={%region_6.7_spmd, %region_7.11_spmd} | conditional | flops 205395968 | bytes 10269464 | solution.py:94
  29.8 0.2 copy.63
  30.0 0.5 reshape.148
  30.5 0.1 and_reduce_fusion
  30.7 0.5 fusion.20
  31.2 0.6 %fusion.2 = f32[64,4,6]{0,2,1:T(8,128)S(1)} fusion(f32[64,4,6,256]{3,0,2,1:T(8,128)S(1)} %get-tuple-element.190, f32[64,4,6]{0,2,1:T(8,128)S(1)} %broadcast_maximum_fusion, pred[64,256]{1,0:T(8,128)(4,1)S(1)} %broadcast_and_fusion), kind=kLoop, calls=%fused_computation.5 | loop fusion | flops 1178112 | bytes 1601536 | tf_op jit(solution)/shard_map/while/body/eval_jaxpr/cond/branch_1_fun/reduce_sum | solution.py:82
  31.7 0.7 %fusion = f32[64,4,6,128]{3,0,2,1:T(8,128)S(1)} fusion(bf16[256,4,128,1]{0,2,3,1:T(8,128)(2,1)S(1)} %bitcast.45, f32[64,4,6,256]{3,0,2,1:T(8,128)S(1)} %get-tuple-element.190, f32[64,4,6,128]{3,0,2,1:T(8,128)S(1)} %get-tuple-element.129, f32[64,4,6]{0,2,1:T(8,128)S(1)} %broadcast_maximum_fusion, pred[64,256]{1,0:T(8,128)(4,1)S(1)} %broadcast_and_fusion, ...), kind=kOutput, calls=%fused_computation.3 | convolution fusion | flops 102236160 | bytes 3436544 | tf_op jit(solution)/shard_map/while/body/eval_jaxpr/cond/branch_1_fun/rkgn,nkd->rkgd/dot_general | solution.py:83
  32.4 0.3 broadcast_divide_fusion
  32.7 0.5 copy.64
  33.2 0.2 reshape.151
  33.4 1.3 %broadcast_select_fusion = (bf16[64,3072]{1,0:T(8,128)(2,1)S(1)}, bf16[64,3072]{1,0:T(8,128)(2,1)}) fusion(pred[]{:T(512)S(6)} %lt.53, f32[64,3072]{1,0:T(8,128)S(1)} %reshape.151, f32[64,3072]{1,0:T(8,128)S(1)} %copy-done, s32[64]{0:T(128)S(1)} %get-tuple-element.181, pred[64]{0:T(512)(128)(4,1)S(1)} %fusion.17), kind=kOutput, calls=%fused_computation.23 | convolution fusion | flops 151785472 | bytes 2359617 | tf_op jit(solution)/shard_map/dot_general | solution.py:129
  34.7 2.7 %collective-permute-start = (bf16[16,3072]{1,0:T(8,128)(2,1)S(1)}, bf16[16,3072]{1,0:T(8,128)(2,1)S(1)}, u32[]{:S(2)}, u32[]{:S(2)}) collective-permute-start(bf16[16,3072]{1,0:T(8,128)(2,1)S(1)} %get-tuple-element.193), channel_id=1, source_target_pairs={{0,24},{1,25},{2,26},{3,27},{4,28},{5,29},{6,30},{7,31}} | collective-permute-start | bytes 294920 | tf_op jit(solution)/shard_map/ppermute | solution.py:17
  37.4 1.3 %collective-permute-start.1 = (bf16[16,3072]{1,0:T(8,128)(2,1)S(1)}, bf16[16,3072]{1,0:T(8,128)(2,1)S(1)}, u32[]{:S(2)}, u32[]{:S(2)}) collective-permute-start(bf16[16,3072]{1,0:T(8,128)(2,1)S(1)} %get-tuple-element.192), channel_id=1, source_target_pairs={{0,16},{8,24},{1,17},{9,25},{2,18},{10,26},{3,19},{11,27},{4,20},{... | collective-permute-start | bytes 294920 | tf_op jit(solution)/shard_map/ppermute | solution.py:17
  38.7 2.0 %collective-permute-start.2 = (bf16[16,3072]{1,0:T(8,128)(2,1)S(1)}, bf16[16,3072]{1,0:T(8,128)(2,1)S(1)}, u32[]{:S(2)}, u32[]{:S(2)}) collective-permute-start(bf16[16,3072]{1,0:T(8,128)(2,1)S(1)} %get-tuple-element.191), channel_id=1, source_target_pairs={{0,8},{8,16},{16,24},{1,9},{9,17},{17,25},{2,10},{10,18},{18,26},{... | collective-permute-start | bytes 294920 | tf_op jit(solution)/shard_map/ppermute | solution.py:17
  40.8 3.5 %all-to-all-start.3 = ((bf16[2,32,3072]{2,1,0:T(8,128)(2,1)}), bf16[2,32,3072]{2,1,0:T(8,128)(2,1)S(1)}, u32[]{:S(2)}, u32[]{:S(2)}) async-start(bf16[2,32,3072]{2,1,0:T(8,128)(2,1)} %bitcast.11), calls=%async_computation.3 | async-start | bytes 786432 | tf_op jit(solution)/shard_map/all_to_all | solution.py:136
  44.3 0.7 %fusion.13 = bf16[16,3072]{1,0:T(8,128)(2,1)} fusion(bf16[16,3072]{1,0:T(8,128)(2,1)S(1)} %collective-permute-done, bf16[16,3072]{1,0:T(8,128)(2,1)S(1)} %collective-permute-done.1, bf16[16,3072]{1,0:T(8,128)(2,1)S(1)} %collective-permute-done.2, bf16[64,3072]{1,0:T(8,128)(2,1)S(1)} %get-tuple-element.196, pred[]{:T(512)S(6)} %eq.97, pred[]{:T(512)S(6)} %eq.96, ...), kind=kLoop, calls=%fused_computation.27 | loop fusion | flops 147456 | bytes 491523 | tf_op jit(solution)/shard_map/jit(_where)/select_n | solution.py:156
  44.9 6.6 %all-to-all-done.3 = bf16[2,32,3072]{2,1,0:T(8,128)(2,1)S(1)} async-done(((bf16[2,32,3072]{2,1,0:T(8,128)(2,1)}), bf16[2,32,3072]{2,1,0:T(8,128)(2,1)S(1)}, u32[]{:S(2)}, u32[]{:S(2)}) %all-to-all-start.3) | async-done | bytes 393248 | tf_op jit(solution)/shard_map/all_to_all | solution.py:136
  51.5 0.8 %copy.75 = bf16[2,4,8,3072]{3,2,0,1:T(8,128)(2,1)} copy(bf16[2,4,8,3072]{3,2,1,0:T(8,128)(2,1)S(1)} %bitcast.43) | data formatting | bytes 786432 | tf_op jit(solution)/shard_map/all_to_all | solution.py:136
  (23 shorter events, 0.3 us)
Async XLA Ops:
  0.6 32.8 %copy-start = (f32[64,3072]{1,0:T(8,128)S(1)}, f32[64,3072]{1,0:T(8,128)}, u32[]{:S(2)}) copy-start(f32[64,3072]{1,0:T(8,128)} %param.12) | copy-start | bytes 2359300
  2.2 8.9 %all-to-all-start.1 = ((bf16[32,2,512]{2,0,1:T(8,128)(2,1)}), bf16[32,2,512]{2,0,1:T(8,128)(2,1)S(1)}, u32[]{:S(2)}, u32[]{:S(2)}) async-start(bf16[32,2,512]{2,0,1:T(8,128)(2,1)} %bitcast.40), calls=%async_computation.1 | async-start | bytes 131072 | tf_op jit(solution)/shard_map/all_to_all | solution.py:34
  11.1 7.4 %all-to-all-start = ((bf16[32,2,512]{2,0,1:T(8,128)(2,1)}), bf16[32,2,512]{2,0,1:T(8,128)(2,1)S(1)}, u32[]{:S(2)}, u32[]{:S(2)}) async-start(bf16[32,2,512]{2,0,1:T(8,128)(2,1)} %bitcast.41), calls=%async_computation | async-start | bytes 131072 | tf_op jit(solution)/shard_map/all_to_all | solution.py:33
  18.5 11.2 %all-to-all-start.2 = ((bf16[32,2,3072]{2,0,1:T(8,128)(2,1)}), bf16[32,2,3072]{2,0,1:T(8,128)(2,1)S(1)}, u32[]{:S(2)}, u32[]{:S(2)}) async-start(bf16[32,2,3072]{2,0,1:T(8,128)(2,1)} %bitcast.39), calls=%async_computation.2 | async-start | bytes 786432 | tf_op jit(solution)/shard_map/all_to_all | solution.py:32
  34.7 9.5 %collective-permute-start = (bf16[16,3072]{1,0:T(8,128)(2,1)S(1)}, bf16[16,3072]{1,0:T(8,128)(2,1)S(1)}, u32[]{:S(2)}, u32[]{:S(2)}) collective-permute-start(bf16[16,3072]{1,0:T(8,128)(2,1)S(1)} %get-tuple-element.193), channel_id=1, source_target_pairs={{0,24},{1,25},{2,26},{3,27},{4,28},{5,29},{6,30},{7,31}} | collective-permute-start | bytes 294920 | tf_op jit(solution)/shard_map/ppermute | solution.py:17
  37.4 6.8 %collective-permute-start.1 = (bf16[16,3072]{1,0:T(8,128)(2,1)S(1)}, bf16[16,3072]{1,0:T(8,128)(2,1)S(1)}, u32[]{:S(2)}, u32[]{:S(2)}) collective-permute-start(bf16[16,3072]{1,0:T(8,128)(2,1)S(1)} %get-tuple-element.192), channel_id=1, source_target_pairs={{0,16},{8,24},{1,17},{9,25},{2,18},{10,26},{3,19},{11,27},{4,20},{... | collective-permute-start | bytes 294920 | tf_op jit(solution)/shard_map/ppermute | solution.py:17
  38.7 5.6 %collective-permute-start.2 = (bf16[16,3072]{1,0:T(8,128)(2,1)S(1)}, bf16[16,3072]{1,0:T(8,128)(2,1)S(1)}, u32[]{:S(2)}, u32[]{:S(2)}) collective-permute-start(bf16[16,3072]{1,0:T(8,128)(2,1)S(1)} %get-tuple-element.191), channel_id=1, source_target_pairs={{0,8},{8,16},{16,24},{1,9},{9,17},{17,25},{2,10},{10,18},{18,26},{... | collective-permute-start | bytes 294920 | tf_op jit(solution)/shard_map/ppermute | solution.py:17
  40.8 10.8 %all-to-all-start.3 = ((bf16[2,32,3072]{2,1,0:T(8,128)(2,1)}), bf16[2,32,3072]{2,1,0:T(8,128)(2,1)S(1)}, u32[]{:S(2)}, u32[]{:S(2)}) async-start(bf16[2,32,3072]{2,1,0:T(8,128)(2,1)} %bitcast.11), calls=%async_computation.3 | async-start | bytes 786432 | tf_op jit(solution)/shard_map/all_to_all | solution.py:136
